TPU v7x, 32 devices: a whole 2x2x4 slice. The times are simulated.
32 devices in a mesh: dp: 8 (over z, y), tensor: 4 (over x, core).
Axes of the slice: x: 2, y: 2, z: 4, core: 2. Of those that a mesh axis runs over, the one named last changes fastest.
Arguments:
- tree_ids: int32 [8, 64], P('dp'), may hold values from 0 to 65535, as said below
- ancestors: int32 [8, 64, 64], P('dp'), may hold values from 0 to 1, as said below
- lengths: int32 [8], P('dp'), may hold values from 64 to 1024, as said below
- table: bfloat16 [65536, 4096], P('dp', 'tensor'), may hold values from -3 to 3
- gain: bfloat16 [4096], replicated, may hold values from 0.25 to 1.75
- w_query: bfloat16 [4096, 4096], P(None, 'tensor'), may hold values from -0.09375 to 0.09375
- w_kv: bfloat16 [2, 4096, 1024], P(None, None, 'tensor'), may hold values from -0.09375 to 0.09375
- w_out: bfloat16 [4096, 4096], P('tensor'), may hold values from -0.09375 to 0.09375
- key_cache: bfloat16 [8, 8, 1024, 128], P('dp', 'tensor'), may hold values from -480 to 480
- value_cache: bfloat16 [8, 8, 1024, 128], P('dp', 'tensor'), may hold values from -6 to 6
Outputs:
- layer_output: bfloat16 [512, 4096], P('dp', 'tensor')
Inputs may be any that keep to these rules, and one draw needn't show every extreme that they name: `tree_ids`: split the vocabulary into equal consecutive parts, one for each index of dp; of the nodes of the rows of one index of dp, at most 16 have ids in any one part, and exactly 16 in some part. Row n of each row's matrix marks node n and all its ancestors in that row's tree; node 0 is the root and every other node's parent has a smaller index. `lengths`: some row has all 1024 slots live.
All inputs are finite; a program needn't handle non-finite values.
Results may differ from a plain program's by a relative error of at most 0.004.
The roundings to bfloat16 on the way count: a program that leaves them out, or rounds other values in their place, can miss the bound.
Values may be sent and summed in bfloat16 or wider, within the bound.
A program may use at most 128 MiB of HBM per device.

v0:
```python
import math
import jax
import jax.numpy as jnp
from jax import lax
from jax.sharding import PartitionSpec as P

D = 4096
EPS = 1e-05
NEG = -1e30
THETA = 500000.0


def rotary(values, positions):
    half_dim = values.shape[-1] // 2
    freq_index = jnp.arange(half_dim, dtype=jnp.float32)
    inverse = jnp.exp(freq_index * (-2.0 * math.log(THETA) / values.shape[-1]))
    angles = positions[:, None] * inverse[None, :]
    cosine = jnp.cos(angles)[:, None, :]
    sine_part = jnp.sin(angles)[:, None, :]
    lower_half = values[..., :half_dim]
    upper_half = values[..., half_dim:]
    return jnp.concatenate(
        [
            lower_half * cosine - upper_half * sine_part,
            upper_half * cosine + lower_half * sine_part,
        ],
        axis=-1,
    )


def contract(left_side, right_side):
    return lax.dot_general(
        left_side, right_side, (((1,), (1,)), ((), ())), preferred_element_type=jnp.float32
    )


def to_groups(tensor_in, kv_heads, head_dim):
    row_count, node_count, width_all = tensor_in.shape
    per_group = width_all // (kv_heads * head_dim)
    grouped = tensor_in.reshape(row_count, node_count, kv_heads, per_group, head_dim).transpose(
        0, 2, 3, 1, 4
    )
    return grouped.reshape(row_count, kv_heads, per_group * node_count, head_dim)


def from_groups(tensor_in, node_count):
    row_count, kv_heads, group_rows, head_dim = tensor_in.shape
    grouped = tensor_in.reshape(row_count, kv_heads, group_rows // node_count, node_count, head_dim)
    return grouped.transpose(0, 3, 1, 2, 4).reshape(row_count, node_count, -1)


def attend(query_group, keys_tree, values_tree, keys_cache, values_cache, live_len, tree_mask):
    score_scale = keys_cache.shape[-1] ** (-0.5)
    slot_count = keys_cache.shape[0]
    cache_scores = contract(query_group, keys_cache) * score_scale
    columns = jnp.arange(slot_count, dtype=jnp.int32)
    cache_scores = jnp.where(columns[None, :] < live_len, cache_scores, NEG)
    tree_scores = contract(query_group, keys_tree) * score_scale
    groups = query_group.shape[0] // tree_mask.shape[0]
    tree_scores = jnp.where(jnp.tile(tree_mask, (groups, 1)) > 0, tree_scores, NEG)
    row_top = jnp.maximum(jnp.max(cache_scores, axis=1), jnp.max(tree_scores, axis=1))[:, None]
    cache_exp = jnp.exp(cache_scores - row_top)
    tree_exp = jnp.exp(tree_scores - row_top)
    denominator = jnp.sum(cache_exp, axis=1) + jnp.sum(tree_exp, axis=1)
    cache_weights = cache_exp.astype(jnp.bfloat16)
    weighted = jnp.dot(
        tree_exp.astype(jnp.bfloat16), values_tree, preferred_element_type=jnp.float32
    )
    weighted = weighted + jnp.dot(cache_weights, values_cache, preferred_element_type=jnp.float32)
    return (weighted / denominator[:, None]).astype(jnp.bfloat16)


def slot_ranks(owner_blocks):
    token_span = owner_blocks.shape[-1]
    positions_here = jnp.arange(token_span, dtype=jnp.int32)
    earlier = positions_here[None, :] < positions_here[:, None]
    same_owner = owner_blocks[..., :, None] == owner_blocks[..., None, :]
    return jnp.sum((same_owner & earlier).astype(jnp.int32), axis=-1)


def shards(tree_ids, ancestors, lengths, table, gain, w_query, w_kv, w_out, key_cache, value_cache):
    row_count, node_count = tree_ids.shape
    token_count = row_count * node_count
    head_dim = key_cache.shape[3]
    kv_local = key_cache.shape[1]
    all_ids = lax.all_gather(tree_ids, "dp", axis=0, tiled=True).reshape(-1)
    vocab_rows = table.shape[0]
    dp_count = lax.axis_size("dp")
    my_index = lax.axis_index("dp")
    capacity = 2 * ((token_count + dp_count - 1) // dp_count)
    block_ids = all_ids.reshape(dp_count, token_count)
    owner_blocks = block_ids // vocab_rows
    ranks = slot_ranks(owner_blocks)
    mine = owner_blocks == my_index
    slot_hit = mine[:, :, None] & (
        ranks[:, :, None] == jnp.arange(capacity, dtype=jnp.int32)[None, None, :]
    )
    token_place = jnp.arange(token_count, dtype=jnp.int32)[None, :, None]
    source_token = jnp.sum(jnp.where(slot_hit, token_place, 0), axis=1)
    slot_used = jnp.any(slot_hit, axis=1)
    source_ids = jnp.take_along_axis(block_ids, source_token, axis=1)
    source_offsets = jnp.clip(source_ids - my_index * vocab_rows, 0, vocab_rows - 1)
    slot_rows = jnp.take(table, source_offsets.reshape(-1), axis=0).reshape(
        dp_count, capacity, table.shape[1]
    )
    slot_rows = jnp.where(slot_used[:, :, None], slot_rows, jnp.zeros((), slot_rows.dtype))
    arrived = lax.all_to_all(slot_rows, "dp", split_axis=0, concat_axis=0, tiled=True)
    own_ids = tree_ids.reshape(-1)
    own_owner = own_ids // vocab_rows
    own_rank = slot_ranks(own_owner)
    flat_slot = own_owner * capacity + own_rank
    embedded = jnp.take(arrived.reshape(dp_count * capacity, table.shape[1]), flat_slot, axis=0)
    gain_full = gain.astype(jnp.float32)
    features = lax.all_gather(embedded, "tensor", axis=1, tiled=True).astype(jnp.float32)
    inv_rms = lax.rsqrt(jnp.sum(features * features, axis=1) / D + EPS)
    normed = (features * inv_rms[:, None] * gain_full[None, :]).astype(jnp.bfloat16)
    queries = jnp.dot(normed, w_query, preferred_element_type=jnp.float32)
    keys_new = jnp.dot(normed, w_kv[0], preferred_element_type=jnp.float32)
    values_raw = jnp.dot(normed, w_kv[1], preferred_element_type=jnp.float32)
    values_new = values_raw.astype(jnp.bfloat16).reshape(row_count, node_count, -1)
    node_depth = jnp.sum(ancestors, axis=2) - 1
    positions = (lengths[:, None] + node_depth).reshape(-1).astype(jnp.float32)
    query_heads = w_query.shape[1] // head_dim
    queries = rotary(queries.reshape(token_count, query_heads, head_dim), positions).astype(
        jnp.bfloat16
    )
    queries = queries.reshape(row_count, node_count, query_heads * head_dim)
    keys_new = rotary(keys_new.reshape(token_count, kv_local, head_dim), positions).astype(
        jnp.bfloat16
    )
    keys_new = keys_new.reshape(row_count, node_count, kv_local * head_dim)
    query_groups = to_groups(queries, kv_local, head_dim)
    key_groups = to_groups(keys_new, kv_local, head_dim)
    value_groups = to_groups(values_new, kv_local, head_dim)

    def per_row(row_items):
        row_q, row_k, row_v, row_kc, row_vc, live_len, tree_mask = row_items

        def per_head(head_items):
            return attend(
                head_items[0],
                head_items[1],
                head_items[2],
                head_items[3],
                head_items[4],
                live_len,
                tree_mask,
            )

        return lax.map(per_head, (row_q, row_k, row_v, row_kc, row_vc))

    contexts = lax.map(
        per_row,
        (query_groups, key_groups, value_groups, key_cache, value_cache, lengths, ancestors),
    )
    contexts = from_groups(contexts, node_count).reshape(token_count, query_heads * head_dim)
    partial_out = jnp.dot(contexts, w_out, preferred_element_type=jnp.float32)
    attention = lax.psum_scatter(partial_out, "tensor", scatter_dimension=1, tiled=True)
    return (embedded.astype(jnp.float32) + attention).astype(jnp.bfloat16)


def solution(mesh):
    in_specs = (
        P("dp", None),
        P("dp", None, None),
        P("dp"),
        P("dp", "tensor"),
        P(),
        P(None, "tensor"),
        P(None, None, "tensor"),
        P("tensor", None),
        P("dp", "tensor", None, None),
        P("dp", "tensor", None, None),
    )
    out_specs = P("dp", "tensor")
    return jax.shard_map(shards, mesh=mesh, in_specs=in_specs, out_specs=out_specs, check_vma=False)
```

profile of v0, /device:TPU:0, one launch (start us, length us, event | category | flops | bytes accessed | tf_op | source)
XLA Modules:
  0.0 113.7 jit_solution(4923900093917061358)
XLA Ops:
  6.5 0.0 copy-start.4
  6.5 22.5 %all-gather = s32[8,1,64]{2,1,0:T(1,128)S(1)} all-gather(s32[1,1,64]{2,1,0:T(1,128)} %bitcast.147), channel_id=1, replica_groups=mesh['dp'=8,'tensor'=4] {'dp'}, dimensions={0}, use_global_device_ids=true | all-gather | bytes 2304 | tf_op jit(solution)/shard_map/all_gather | solution.py:86
  29.0 0.3 convert_reduce_fusion
  29.4 0.2 select_reduce_fusion
  29.6 0.1 reduce_sum.73
  29.7 0.2 fusion.43
  29.9 0.1 reshape.421
  30.0 1.0 gather_fusion.2
  31.0 0.0 copy-start.2
  31.0 0.0 copy-start.3
  31.0 0.1 reshape.424
  31.1 9.0 %gather_fusion = bf16[128,1024]{1,0:T(8,128)(2,1)S(1)} fusion(bf16[8192,1024]{1,0:T(8,128)(2,1)} %param.15, s32[1024]{0:T(1024)S(1)} %pad_clamp_fusion.1), kind=kCustom, calls=%fused_computation | custom fusion | bytes 524800 | tf_op jit(solution)/shard_map/jit(_take)/gather | solution.py:103
  40.1 0.8 select_select_fusion
  41.0 3.4 %all-to-all-start = ((bf16[8,16,1024]{2,1,0:T(8,128)(2,1)}), bf16[8,16,1024]{2,1,0:T(8,128)(2,1)S(1)}, u32[]{:S(2)}, u32[]{:S(2)}) async-start(bf16[8,16,1024]{2,1,0:T(8,128)(2,1)} %select_select_fusion), calls=%async_computation | async-start | bytes 524288 | tf_op jit(solution)/shard_map/all_to_all | solution.py:107
  44.4 0.0 reduce-scatter.2.cloned.1.call-start
  44.4 0.0 copy-done.4
  44.5 0.2 convert_reduce_fusion.1
  44.7 3.1 %slice_bitcast_fusion = bf16[256,4096]{0,1:T(8,128)(2,1)} fusion(bf16[2,4096,256]{2,1,0:T(8,128)(2,1)} %param.18), kind=kLoop, calls=%fused_computation.42 | loop fusion | bytes 4194304 | tf_op jit(solution)/shard_map/dot_general | solution.py:118
  48.4 0.0 copy-done.2
  48.4 0.1 reduce_sum.76
  48.6 0.1 copy.29
  48.6 0.0 copy-done.3
  48.7 2.9 %copy.32 = bf16[256,4096]{1,0:T(8,128)(2,1)S(1)} copy(bf16[256,4096]{0,1:T(8,128)(2,1)} %slice_bitcast_fusion) | data formatting | bytes 4194304 | tf_op jit(solution)/shard_map/dot_general | solution.py:118
  51.6 0.2 multiply_cosine_fusion
  51.8 0.7 all-to-all-done
  52.5 0.7 gather_fusion.1
  53.2 0.1 broadcast_select_fusion
  53.3 7.2 %all_gather.7 = bf16[64,4096]{1,0:T(8,128)(2,1)S(1)} all-gather(bf16[64,1024]{1,0:T(8,128)(2,1)S(1)} %broadcast_select_fusion), channel_id=1, replica_groups=mesh['dp'=8,'tensor'=4] {'tensor'}, dimensions={1}, use_global_device_ids=true | all-gather | bytes 655360 | tf_op jit(solution)/shard_map/all_gather | solution.py:114
  60.5 0.2 fusion.37
  60.7 2.1 %fusion.34 = bf16[64,256]{1,0:T(8,128)(2,1)S(1)} fusion(bf16[2,4096,256]{2,1,0:T(8,128)(2,1)} %param.18, bf16[64,4096]{1,0:T(8,128)(2,1)S(1)} %all_gather.7, f32[4096]{0:T(1024)S(1)} %convert_element_type.60, f32[64]{0:T(128)S(1)} %add_rsqrt_fusion), kind=kOutput, calls=%fused_computation.46 | convolution fusion | flops 135282688 | bytes 2670848 | tf_op jit(solution)/shard_map/dot_general | solution.py:119
  62.8 0.8 fusion.40
  63.6 0.0 copy-start
  63.6 0.0 copy-start.1
  63.7 5.1 %convolution_bitcast_fusion = f32[8,8,8,128]{3,1,2,0:T(8,128)S(1)} fusion(bf16[4096,1024]{1,0:T(8,128)(2,1)} %param.17, bf16[64,4096]{1,0:T(8,128)(2,1)S(1)} %all_gather.7, f32[4096]{0:T(1024)S(1)} %convert_element_type.60, f32[64]{0:T(128)S(1)} %add_rsqrt_fusion), kind=kOutput, calls=%fused_computation.45 | convolution fusion | flops 537919488 | bytes 9191680 | tf_op jit(solution)/shard_map/dot_general | solution.py:117
  68.8 0.1 fusion.44
  68.9 0.2 subtract_convert_fusion
  69.1 0.1 pad_maximum_fusion
  69.2 0.1 maximum_bitcast_fusion
  69.3 0.0 copy-done
  69.3 0.0 copy-done.1
  69.4 4.8 %while.17 = (s32[]{:T(128)}, bf16[2,256,128]{2,1,0:T(8,128)(2,1)S(1)}, s32[64,64]{0,1:T(8,128)S(1)}, bf16[2,256,128]{2,1,0:T(8,128)(2,1)S(1)}, bf16[2,64,128]{2,...) while((s32[]{:T(128)}, ...), condition=%wide.region_11.12_spmd, body=%wide.region_6.11_spmd.sunk | while | flops 144658944 | bytes 4468845 | solution.py:150
  69.4 0.7 iota_compare_fusion.4
  70.0 0.4 fusion.79
  70.5 0.1 gt.11
  70.6 0.2 fusion.78
  70.8 0.3 fusion.81
  71.1 0.2 fusion.80
  71.3 0.4 fusion.83
  71.7 0.7 iota_compare_fusion.4
  72.4 0.4 fusion.79
  72.8 0.1 gt.11
  73.0 0.2 fusion.78
  73.2 0.3 fusion.81
  73.5 0.2 fusion.80
  73.7 0.4 fusion.83
  74.1 0.1 copy.38
  74.2 0.1 reshape_reshape.9
  74.3 5.9 %fusion.59 = f32[64,4096]{1,0:T(8,128)} fusion(bf16[64,1024]{1,0:T(8,128)(2,1)S(1)} %reshape_reshape.9, bf16[1024,4096]{1,0:T(8,128)(2,1)} %param.19), kind=kOutput, calls=%fused_computation.120 | convolution fusion | flops 536870912 | bytes 9568256 | tf_op jit(solution)/shard_map/dot_general | solution.py:157
  80.2 0.0 reduce-scatter.2.cloned.1.call-update
  80.3 24.9 %reduce-scatter.2.cloned.1.call-done = f32[64,1024]{1,0:T(8,128)} async-done(((f32[64,4096]{1,0:T(8,128)}), f32[64,1024]{1,0:T(8,128)}) %reduce-scatter.2.cloned.1.call-update) | async-done | bytes 262160 | tf_op jit(solution)/shard_map/reduce_scatter | solution.py:158
  105.1 1.7 %add_convert_fusion = bf16[64,1024]{1,0:T(8,128)(2,1)} fusion(f32[64,1024]{1,0:T(8,128)} %reduce-scatter.2.cloned.1.call-done, bf16[64,1024]{1,0:T(8,128)(2,1)S(1)} %gather_fusion.1, pred[64]{0:T(512)(128)(4,1)S(1)} %compare_and_fusion.1), kind=kLoop, calls=%fused_computation.52 | loop fusion | flops 262144 | bytes 524352 | tf_op jit(solution)/shard_map/convert_element_type | solution.py:159
  (30 shorter events, 0.4 us)
Async XLA Ops:
  6.5 37.9 %copy-start.4 = (s32[1,64]{1,0:T(1,128)S(1)}, s32[1,64]{1,0:T(1,128)}, u32[]{:S(2)}) copy-start(s32[1,64]{1,0:T(1,128)} %param.12) | copy-start | bytes 772
  31.0 17.4 %copy-start.2 = (s32[1,64,64]{2,1,0:T(8,128)S(1)}, s32[1,64,64]{2,1,0:T(8,128)}, u32[]{:S(2)}) copy-start(s32[1,64,64]{2,1,0:T(8,128)} %param.13) | copy-start | bytes 49156
  31.0 17.6 %copy-start.3 = (bf16[4096]{0:T(1024)(128)(2,1)S(1)}, bf16[4096]{0:T(1024)(128)(2,1)}, u32[]{:S(2)}) copy-start(bf16[4096]{0:T(1024)(128)(2,1)} %param.16) | copy-start | bytes 24580
  41.0 11.6 %all-to-all-start = ((bf16[8,16,1024]{2,1,0:T(8,128)(2,1)}), bf16[8,16,1024]{2,1,0:T(8,128)(2,1)S(1)}, u32[]{:S(2)}, u32[]{:S(2)}) async-start(bf16[8,16,1024]{2,1,0:T(8,128)(2,1)} %select_select_fusion), calls=%async_computation | async-start | bytes 524288 | tf_op jit(solution)/shard_map/all_to_all | solution.py:107
  44.4 60.8 %reduce-scatter.2.cloned.1.call-start = ((), (), s32[]{:S(2)}) async-start(), calls=%async_computation.2 | async-start | bytes 1310720 | tf_op jit(solution)/shard_map/reduce_scatter | solution.py:158
  63.6 5.7 %copy-start = (bf16[1,2,1024,128]{3,2,1,0:T(8,128)(2,1)S(1)}, bf16[1,2,1024,128]{3,2,1,0:T(8,128)(2,1)}, u32[]{:S(2)}) copy-start(bf16[1,2,1024,128]{3,2,1,0:T(8,128)(2,1)} %param.21) | copy-start | bytes 1572868
  63.6 5.7 %copy-start.1 = (bf16[1,2,1024,128]{3,2,1,0:T(8,128)(2,1)S(1)}, bf16[1,2,1024,128]{3,2,1,0:T(8,128)(2,1)}, u32[]{:S(2)}) copy-start(bf16[1,2,1024,128]{3,2,1,0:T(8,128)(2,1)} %param.20) | copy-start | bytes 1572868
Sparse Core Ops, SparseCore 0:
  80.4 24.6 reduce-scatter.1
where the time goes:
time: 114 us
  blocking collectives  29.6 us (26%)
  waiting for transfers between devices  25.6 us (22%)
  local copies, waits for them, and re-layouts  17.6 us (15%)
  matrix products  16.2 us (14%)
  between operations  14.3 us (13%)
  other arithmetic  6.69 us (6%)
  starting transfers between devices  3.45 us (3%)
    reduce_scatter x1, waiting for transfers between devices, shards(): lax.psum_scatter(partial_out, 'tensor', scatter_dimension=1, tiled=True)  24.9 us
    all_gather x1, blocking collectives, shards(): all_ids = lax.all_gather(tree_ids, 'dp', axis=0, tiled=True).reshape(-1)  22.5 us
    gather x1, local copies, waits for them, and re-layouts, shards(): jnp.take(table, source_offsets.reshape(-1), axis=0)  8.97 us
    all_gather x1, blocking collectives, shards(): lax.all_gather(embedded, 'tensor', axis=1, tiled=True).astype(jnp.float32)  7.17 us
    dot_general x2, local copies, waits for them, and re-layouts, shards(): keys_new = jnp.dot(normed, w_kv[0], preferred_element_type=jnp.float32)  6 us
    dot_general x1, matrix products, shards(): partial_out = jnp.dot(contexts, w_out, preferred_element_type=jnp.float32)  5.94 us
    dot_general x1, matrix products, shards(): queries = jnp.dot(normed, w_query, preferred_element_type=jnp.float32)  5.09 us
    all_to_all x1, starting transfers between devices, shards(): lax.all_to_all(slot_rows, 'dp', split_axis=0, concat_axis=0, tiled=True)  3.41 us
  transfers between devices with their start and end apart: 2, of which 2 were waited for; matrix products, arithmetic and copies ran while one was open for 6% of the time, Pallas kernels for 0%

commit v1 on v0

--- a/solution.py
+++ b/solution.py
@@ -8,6 +8,19 @@
 EPS = 1e-05
 NEG = -1e30
 THETA = 500000.0
+
+
+def gather_around(value, axis, dim):
+    ways = lax.axis_size(axis)
+    up = [(d, (d + 1) % ways) for d in range(ways)]
+    down = [(d, (d - 1) % ways) for d in range(ways)]
+    earlier, later = ([value], [value])
+    for _ in range(ways // 2):
+        earlier.append(lax.ppermute(earlier[-1], axis, up))
+    for _ in range((ways - 1) // 2):
+        later.append(lax.ppermute(later[-1], axis, down))
+    line = jnp.concatenate([*earlier[::-1], *later[1:]], axis=dim)
+    return jnp.roll(line, (lax.axis_index(axis) - ways // 2) * value.shape[dim], axis=dim)
 
 
 def rotary(values, positions):
@@ -111,7 +124,7 @@
     flat_slot = own_owner * capacity + own_rank
     embedded = jnp.take(arrived.reshape(dp_count * capacity, table.shape[1]), flat_slot, axis=0)
     gain_full = gain.astype(jnp.float32)
-    features = lax.all_gather(embedded, "tensor", axis=1, tiled=True).astype(jnp.float32)
+    features = gather_around(embedded, "tensor", 1).astype(jnp.float32)
     inv_rms = lax.rsqrt(jnp.sum(features * features, axis=1) / D + EPS)
     normed = (features * inv_rms[:, None] * gain_full[None, :]).astype(jnp.bfloat16)
     queries = jnp.dot(normed, w_query, preferred_element_type=jnp.float32)

time: 114 us -> 118 us (1.035)
  waiting for transfers between devices: 25.6 us -> 33.3 us
  blocking collectives: 29.6 us -> 22.5 us
  starting transfers between devices: 3.45 us -> 5.25 us
  matrix products: 16.2 us -> 17.5 us
    all_gather x1 -> x0, blocking collectives: 7.17 us -> none  [shards(): lax.all_gather(embedded, 'tensor', axis=1, tiled=True).astype(jnp.float32)]
    all_to_all x1, waiting for transfers between devices: 0.73 us -> 5.33 us  [shards(): lax.all_to_all(slot_rows, 'dp', split_axis=0, concat_axis=0, tiled=True)]
    ppermute x0 -> x3, waiting for transfers between devices: none -> 4.34 us  [the longest x2 3.95 us: gather_around(): earlier.append(lax.ppermute(earlier[-1], axis, up))]
    ppermute x0 -> x3, starting transfers between devices: none -> 1.8 us  [the longest x1 1.69 us: gather_around(): later.append(lax.ppermute(later[-1], axis, down))]
    dot_general x2, local copies, waits for them, and re-layouts: 6 us -> 4.66 us  [shards(): keys_new = jnp.dot(normed, w_kv[0], preferred_element_type=jnp.float32)]
    reduce_scatter x1, waiting for transfers between devices: 24.9 us -> 23.6 us  [shards(): lax.psum_scatter(partial_out, 'tensor', scatter_dimension=1, tiled=True)]
    dot_general x2, matrix products: 0.78 us -> 2 us  [attend(): jnp.dot(cache_weights, values_cache, preferred_element_type=jnp.float32)]
  transfers between devices with their start and end apart: 2 -> 5, of which waited for: 2 -> 5; matrix products, arithmetic and copies ran while one was open for 6% -> 5% of each run, Pallas kernels for 0% -> 0%
where the time goes in v1:
time: 118 us
  waiting for transfers between devices  33.3 us (28%)
  blocking collectives  22.5 us (19%)
  matrix products  17.5 us (15%)
  local copies, waits for them, and re-layouts  17.3 us (15%)
  between operations  14.4 us (12%)
  other arithmetic  7.49 us (6%)
  starting transfers between devices  5.25 us (4%)
    reduce_scatter x1, waiting for transfers between devices, shards(): lax.psum_scatter(partial_out, 'tensor', scatter_dimension=1, tiled=True)  23.6 us
    all_gather x1, blocking collectives, shards(): all_ids = lax.all_gather(tree_ids, 'dp', axis=0, tiled=True).reshape(-1)  22.5 us
    gather x1, local copies, waits for them, and re-layouts, shards(): jnp.take(table, source_offsets.reshape(-1), axis=0)  8.97 us
    dot_general x1, matrix products, shards(): partial_out = jnp.dot(contexts, w_out, preferred_element_type=jnp.float32)  5.94 us
    all_to_all x1, waiting for transfers between devices, shards(): lax.all_to_all(slot_rows, 'dp', split_axis=0, concat_axis=0, tiled=True)  5.33 us
    dot_general x1, matrix products, shards(): queries = jnp.dot(normed, w_query, preferred_element_type=jnp.float32)  5.09 us
    dot_general x2, local copies, waits for them, and re-layouts, shards(): keys_new = jnp.dot(normed, w_kv[0], preferred_element_type=jnp.float32)  4.66 us
    ppermute x2, waiting for transfers between devices, gather_around(): earlier.append(lax.ppermute(earlier[-1], axis, up))  3.95 us
  transfers between devices with their start and end apart: 5, of which 5 were waited for; matrix products, arithmetic and copies ran while one was open for 5% of the time, Pallas kernels for 0%

profile of v1, /device:TPU:0, one launch (start us, length us, event | category | flops | bytes accessed | tf_op | source)
XLA Modules:
  0.0 117.6 jit_solution(3881327868106190758)
XLA Ops:
  6.6 22.5 %all-gather = s32[8,1,64]{2,1,0:T(1,128)S(1)} all-gather(s32[1,1,64]{2,1,0:T(1,128)} %bitcast.147), channel_id=1, replica_groups=mesh['dp'=8,'tensor'=4] {'dp'}, dimensions={0}, use_global_device_ids=true | all-gather | bytes 2304 | tf_op jit(solution)/shard_map/all_gather | solution.py:99
  29.0 0.3 convert_reduce_fusion
  29.4 0.2 select_reduce_fusion
  29.6 0.1 reduce_sum.73
  29.7 0.2 fusion.43
  29.9 0.1 reshape.421
  30.0 1.0 gather_fusion.2
  31.0 0.0 copy-start.3
  31.0 0.1 reshape.424
  31.1 0.0 copy-start.4
  31.1 9.0 %gather_fusion = bf16[128,1024]{1,0:T(8,128)(2,1)S(1)} fusion(bf16[8192,1024]{1,0:T(8,128)(2,1)} %param.15, s32[1024]{0:T(1024)S(1)} %pad_clamp_fusion.1), kind=kCustom, calls=%fused_computation | custom fusion | bytes 524800 | tf_op jit(solution)/shard_map/jit(_take)/gather | solution.py:116
  40.1 0.8 select_select_fusion
  40.9 3.4 %all-to-all-start = ((bf16[8,16,1024]{2,1,0:T(8,128)(2,1)}), bf16[8,16,1024]{2,1,0:T(8,128)(2,1)S(1)}, u32[]{:S(2)}, u32[]{:S(2)}) async-start(bf16[8,16,1024]{2,1,0:T(8,128)(2,1)} %select_select_fusion), calls=%async_computation | async-start | bytes 524288 | tf_op jit(solution)/shard_map/all_to_all | solution.py:120
  44.3 0.0 reduce-scatter.2.cloned.1.call-start
  44.4 0.0 copy-done.5
  44.4 1.7 %slice_bitcast_fusion = bf16[256,4096]{0,1:T(8,128)(2,1)S(1)} fusion(bf16[2,4096,256]{2,1,0:T(8,128)(2,1)} %param.18), kind=kLoop, calls=%fused_computation.42 | loop fusion | bytes 4194304 | tf_op jit(solution)/shard_map/dot_general | solution.py:131
  46.8 0.2 convert_reduce_fusion.1
  47.0 0.1 reduce_sum.76
  47.2 5.3 %all-to-all-done = bf16[8,16,1024]{2,1,0:T(8,128)(2,1)S(1)} async-done(((bf16[8,16,1024]{2,1,0:T(8,128)(2,1)}), bf16[8,16,1024]{2,1,0:T(8,128)(2,1)S(1)}, u32[]{:S(2)}, u32[]{:S(2)}) %all-to-all-start) | async-done | bytes 262176 | tf_op jit(solution)/shard_map/all_to_all | solution.py:120
  52.5 0.7 gather_fusion.1
  53.2 0.7 broadcast_select_fusion
  53.9 0.0 collective-permute-start
  54.0 0.1 copy.29
  54.1 2.9 %copy.32 = bf16[256,4096]{1,0:T(8,128)(2,1)} copy(bf16[256,4096]{0,1:T(8,128)(2,1)S(1)} %slice_bitcast_fusion) | data formatting | bytes 4194304 | tf_op jit(solution)/shard_map/dot_general | solution.py:131
  57.0 1.6 %collective-permute-done = bf16[64,1024]{1,0:T(8,128)(2,1)S(1)} collective-permute-done((bf16[64,1024]{1,0:T(8,128)(2,1)}, bf16[64,1024]{1,0:T(8,128)(2,1)S(1)}, u32[]{:S(2)}, u32[]{:S(2)}) %collective-permute-start) | collective-permute-done | bytes 131104 | tf_op jit(solution)/shard_map/ppermute | solution.py:19
  58.6 0.1 collective-permute-start.1
  58.7 0.2 multiply_cosine_fusion
  58.9 1.7 %collective-permute-start.2 = (bf16[64,1024]{1,0:T(8,128)(2,1)}, bf16[64,1024]{1,0:T(8,128)(2,1)S(1)}, u32[]{:S(2)}, u32[]{:S(2)}) collective-permute-start(bf16[64,1024]{1,0:T(8,128)(2,1)} %broadcast_select_fusion), channel_id=1, source_target_pairs={{0,3},{1,0},{2,1},{3,2},{4,7},{5,4},{6,5},{7,6},{8,11},{9,8},{10,9... | collective-permute-start | bytes 393224 | tf_op jit(solution)/shard_map/ppermute | solution.py:21
  60.5 2.4 %collective-permute-done.1 = bf16[64,1024]{1,0:T(8,128)(2,1)S(1)} collective-permute-done((bf16[64,1024]{1,0:T(8,128)(2,1)S(1)}, bf16[64,1024]{1,0:T(8,128)(2,1)S(1)}, u32[]{:S(2)}, u32[]{:S(2)}) %collective-permute-start.1) | collective-permute-done | bytes 131104 | tf_op jit(solution)/shard_map/ppermute | solution.py:19
  63.0 0.1 constant_dynamic-update-slice_fusion.5
  63.1 0.4 collective-permute-done.2
  63.5 0.1 constant_dynamic-update-slice_fusion.1
  63.6 0.2 fusion.37
  63.9 2.1 %fusion.34 = bf16[64,256]{1,0:T(8,128)(2,1)S(1)} fusion(bf16[2,4096,256]{2,1,0:T(8,128)(2,1)} %param.18, f32[4096]{0:T(1024)S(1)} %convert_element_type.60, f32[64]{0:T(128)S(1)} %add_rsqrt_fusion, bf16[64,8192]{1,0:T(8,128)(2,1)S(1)} %constant_dynamic-update-slice_fusion, s32[]{:T(128)S(6)} %select_n.160), kind=kOutput, calls=%fused_computation.46 | convolution fusion | flops 135282688 | bytes 2671108 | tf_op jit(solution)/shard_map/dot_general | solution.py:132
  66.0 0.0 copy-done
  66.0 0.8 fusion.40
  66.8 0.0 copy-start.1
  66.8 0.0 copy-start.2
  66.8 5.1 %convolution_bitcast_fusion = f32[8,8,8,128]{3,1,2,0:T(8,128)S(1)} fusion(bf16[4096,1024]{1,0:T(8,128)(2,1)} %param.17, f32[4096]{0:T(1024)S(1)} %convert_element_type.60, f32[64]{0:T(128)S(1)} %add_rsqrt_fusion, bf16[64,8192]{1,0:T(8,128)(2,1)S(1)} %constant_dynamic-update-slice_fusion, s32[]{:T(128)S(6)} %select_n.160), kind=kOutput, calls=%fused_computation.45 | convolution fusion | flops 537919488 | bytes 9191940 | tf_op jit(solution)/shard_map/dot_general | solution.py:130
  72.0 0.1 fusion.44
  72.1 0.2 subtract_convert_fusion
  72.3 0.1 pad_maximum_fusion
  72.4 0.1 maximum_bitcast_fusion
  72.5 6.0 %while.17 = (s32[]{:T(128)}, bf16[2,256,128]{2,1,0:T(8,128)(2,1)}, s32[64,64]{0,1:T(8,128)S(1)}, bf16[2,256,128]{2,1,0:T(8,128)(2,1)S(1)}, bf16[2,64,128]{2,1,0:...) while((s32[]{:T(128)}, bf16[2,256,128]{2,1,0:T(8,128)(2,1)}, ...), condition=%wide.region_11.12_spmd, body=%wide.region_6.11_spmd.sunk | while | flops 144658944 | bytes 4468845 | solution.py:163
  72.5 0.7 iota_compare_fusion.4
  73.2 0.4 fusion.79
  73.6 0.1 gt.11
  73.8 0.2 fusion.78
  73.9 0.3 fusion.81
  74.3 0.2 fusion.80
  74.5 1.0 fusion.83
  75.5 0.6 iota_compare_fusion.4
  76.2 0.4 fusion.79
  76.6 0.1 gt.11
  76.7 0.2 fusion.78
  76.9 0.3 fusion.81
  77.3 0.2 fusion.80
  77.5 1.0 fusion.83
  78.5 1.0 copy.38
  79.5 0.1 reshape_reshape.9
  79.6 5.9 %fusion.59 = f32[64,4096]{1,0:T(8,128)} fusion(bf16[64,1024]{1,0:T(8,128)(2,1)S(1)} %reshape_reshape.9, bf16[1024,4096]{1,0:T(8,128)(2,1)} %param.19), kind=kOutput, calls=%fused_computation.128 | convolution fusion | flops 536870912 | bytes 9568256 | tf_op jit(solution)/shard_map/dot_general | solution.py:170
  85.5 0.0 reduce-scatter.2.cloned.1.call-update
  85.5 23.6 %reduce-scatter.2.cloned.1.call-done = f32[64,1024]{1,0:T(8,128)} async-done(((f32[64,4096]{1,0:T(8,128)}), f32[64,1024]{1,0:T(8,128)}) %reduce-scatter.2.cloned.1.call-update) | async-done | bytes 262160 | tf_op jit(solution)/shard_map/reduce_scatter | solution.py:171
  109.1 1.7 %add_convert_fusion = bf16[64,1024]{1,0:T(8,128)(2,1)} fusion(f32[64,1024]{1,0:T(8,128)} %reduce-scatter.2.cloned.1.call-done, bf16[64,1024]{1,0:T(8,128)(2,1)S(1)} %gather_fusion.1, pred[64]{0:T(512)(128)(4,1)S(1)} %compare_and_fusion.1), kind=kLoop, calls=%fused_computation.52 | loop fusion | flops 262144 | bytes 524352 | tf_op jit(solution)/shard_map/convert_element_type | solution.py:172
  (42 shorter events, 0.5 us)
Async XLA Ops:
  6.5 37.9 %copy-start.5 = (s32[1,64]{1,0:T(1,128)S(1)}, s32[1,64]{1,0:T(1,128)}, u32[]{:S(2)}) copy-start(s32[1,64]{1,0:T(1,128)} %param.12) | copy-start | bytes 772
  31.0 16.0 %copy-start.3 = (s32[1,64,64]{2,1,0:T(8,128)S(1)}, s32[1,64,64]{2,1,0:T(8,128)}, u32[]{:S(2)}) copy-start(s32[1,64,64]{2,1,0:T(8,128)} %param.13) | copy-start | bytes 49156
  31.1 22.9 %copy-start.4 = (bf16[4096]{0:T(1024)(128)(2,1)S(1)}, bf16[4096]{0:T(1024)(128)(2,1)}, u32[]{:S(2)}) copy-start(bf16[4096]{0:T(1024)(128)(2,1)} %param.16) | copy-start | bytes 24580
  40.9 11.6 %all-to-all-start = ((bf16[8,16,1024]{2,1,0:T(8,128)(2,1)}), bf16[8,16,1024]{2,1,0:T(8,128)(2,1)S(1)}, u32[]{:S(2)}, u32[]{:S(2)}) async-start(bf16[8,16,1024]{2,1,0:T(8,128)(2,1)} %select_select_fusion), calls=%async_computation | async-start | bytes 524288 | tf_op jit(solution)/shard_map/all_to_all | solution.py:120
  44.3 64.8 %reduce-scatter.2.cloned.1.call-start = ((), (), s32[]{:S(2)}) async-start(), calls=%async_computation.2 | async-start | bytes 1310720 | tf_op jit(solution)/shard_map/reduce_scatter | solution.py:171
  53.9 4.6 %collective-permute-start = (bf16[64,1024]{1,0:T(8,128)(2,1)}, bf16[64,1024]{1,0:T(8,128)(2,1)S(1)}, u32[]{:S(2)}, u32[]{:S(2)}) collective-permute-start(bf16[64,1024]{1,0:T(8,128)(2,1)} %broadcast_select_fusion), channel_id=1, source_target_pairs={{0,1},{1,2},{2,3},{3,0},{4,5},{5,6},{6,7},{7,4},{8,9},{9,10},{10,1... | collective-permute-start | bytes 393224 | tf_op jit(solution)/shard_map/ppermute | solution.py:19
  57.0 9.0 %copy-start = (bf16[256,4096]{1,0:T(8,128)(2,1)S(1)}, bf16[256,4096]{1,0:T(8,128)(2,1)}, u32[]{:S(2)}) copy-start(bf16[256,4096]{1,0:T(8,128)(2,1)} %copy.32) | copy-start | bytes 6291460
  58.6 4.4 %collective-permute-start.1 = (bf16[64,1024]{1,0:T(8,128)(2,1)S(1)}, bf16[64,1024]{1,0:T(8,128)(2,1)S(1)}, u32[]{:S(2)}, u32[]{:S(2)}) collective-permute-start(bf16[64,1024]{1,0:T(8,128)(2,1)S(1)} %collective-permute-done), channel_id=1, source_target_pairs={{0,1},{1,2},{2,3},{3,0},{4,5},{5,6},{6,7},{7,4},{8,9},{9,10},{10,1... | collective-permute-start | bytes 393224 | tf_op jit(solution)/shard_map/ppermute | solution.py:19
  58.9 4.6 %collective-permute-start.2 = (bf16[64,1024]{1,0:T(8,128)(2,1)}, bf16[64,1024]{1,0:T(8,128)(2,1)S(1)}, u32[]{:S(2)}, u32[]{:S(2)}) collective-permute-start(bf16[64,1024]{1,0:T(8,128)(2,1)} %broadcast_select_fusion), channel_id=1, source_target_pairs={{0,3},{1,0},{2,1},{3,2},{4,7},{5,4},{6,5},{7,6},{8,11},{9,8},{10,9... | collective-permute-start | bytes 393224 | tf_op jit(solution)/shard_map/ppermute | solution.py:21
  66.8 5.7 %copy-start.1 = (bf16[1,2,1024,128]{3,2,1,0:T(8,128)(2,1)S(1)}, bf16[1,2,1024,128]{3,2,1,0:T(8,128)(2,1)}, u32[]{:S(2)}) copy-start(bf16[1,2,1024,128]{3,2,1,0:T(8,128)(2,1)} %param.21) | copy-start | bytes 1572868
  66.8 5.7 %copy-start.2 = (bf16[1,2,1024,128]{3,2,1,0:T(8,128)(2,1)S(1)}, bf16[1,2,1024,128]{3,2,1,0:T(8,128)(2,1)}, u32[]{:S(2)}) copy-start(bf16[1,2,1024,128]{3,2,1,0:T(8,128)(2,1)} %param.20) | copy-start | bytes 1572868
Sparse Core Ops, SparseCore 0:
  85.6 23.4 reduce-scatter.1
